TPU v7x, 256 devices: a whole 4x4x8 slice. The times are simulated.
256 devices in a mesh: blk: 16 (over z, core), red: 16 (over x, y).
Axes of the slice: x: 4, y: 4, z: 8, core: 2. Of those that a mesh axis runs over, the one named last changes fastest.
Arguments:
- amplitudes: bfloat16 [8, 192, 128, 128], P(None, 'blk', 'red'), may hold values from -6 to 6
- ladder_ints: bfloat16 [16384, 16384], P('red', 'blk'), may hold values from -0.046875 to 0.046875
- cycle_ints: bfloat16 [24576, 24576], P('blk', 'red'), may hold values from -0.0390625 to 0.0390625
- occ_energy: float32 [192], replicated, may hold values from -2 to -0.3
- vir_energy: float32 [128], replicated, may hold values from 0.2 to 3
- slab_index: int32 [8], replicated, may hold values from 0 to 191
Outputs:
- update: float32 [8, 192, 128, 128], P(None, 'red', 'blk')
All inputs are finite; a program needn't handle non-finite values.
Results may differ from a plain program's by a relative error of at most 0.0003.
Values may be sent and summed in bfloat16 or wider, within the bound.
A program may use at most 64 MiB of HBM per device.

v0:
```python
import jax
import jax.numpy as jnp
from jax import lax
from jax.sharding import PartitionSpec as P


def shards(amplitudes, ladder_ints, cycle_ints, occ_energy, vir_energy, slab_index):
    slab_rows, occ_local, vir_local, virt_width = amplitudes.shape
    occ_all = occ_local * lax.axis_size("blk")
    occ_red = occ_all // lax.axis_size("red")
    shard_piece = lax.all_gather(amplitudes, "blk", axis=1, tiled=True)
    row_count = shard_piece.shape[1]
    flattened = shard_piece.reshape(slab_rows * row_count, vir_local * virt_width)
    product = jnp.dot(flattened, ladder_ints, preferred_element_type=jnp.float32)
    ladder = product.reshape(slab_rows, row_count, ladder_ints.shape[1])
    ladder_own = lax.psum_scatter(ladder, "red", scatter_dimension=1, tiled=True)
    ladder_own = ladder_own.reshape(slab_rows, occ_red, -1, virt_width)
    shard_piece = lax.all_gather(amplitudes, "red", axis=2, tiled=True)
    vir_count = shard_piece.shape[2]
    operand = jnp.transpose(shard_piece, (0, 2, 1, 3)).reshape(
        slab_rows * vir_count, occ_local * virt_width
    )
    product = jnp.dot(operand, cycle_ints, preferred_element_type=jnp.float32)
    cycle_term = product.reshape(slab_rows, vir_count, cycle_ints.shape[1])
    cycle_own = lax.psum_scatter(cycle_term, "blk", scatter_dimension=1, tiled=True)
    vir_block = cycle_own.shape[1]
    cycle_own = jnp.transpose(
        cycle_own.reshape(slab_rows, vir_block, occ_red, virt_width), (0, 2, 1, 3)
    )
    orbital_ids = jnp.arange(occ_energy.shape[0], dtype=jnp.int32)
    chosen = slab_index[:, None] == orbital_ids[None, :]
    slab_energy = jnp.sum(jnp.where(chosen, occ_energy[None, :], jnp.float32(0.0)), axis=1)
    pair_energy = lax.dynamic_slice_in_dim(occ_energy, lax.axis_index("red") * occ_red, occ_red)
    first_virtual = lax.dynamic_slice_in_dim(
        vir_energy, lax.axis_index("blk") * vir_block, vir_block
    )
    denominator = (
        first_virtual[None, None, :, None]
        + vir_energy[None, None, None, :]
        - slab_energy[:, None, None, None]
        - pair_energy[None, :, None, None]
    )
    return (ladder_own + cycle_own) / denominator


def solution(mesh):
    placed = (P(None, "blk", "red", None), P("red", "blk"), P("blk", "red"), P(), P(), P())
    return jax.shard_map(
        shards, mesh=mesh, in_specs=placed, out_specs=P(None, "red", "blk", None), check_vma=False
    )
```

profile of v0, /device:TPU:1, one launch (start us, length us, event | category | flops | bytes accessed | tf_op | source)
XLA Modules:
  0.0 272.5 jit_solution(8363558085387435878)
XLA Ops:
  6.5 0.0 copy-start
  6.5 0.0 all-gather.5.cloned.1.call-start
  6.5 1.8 copy.20
  8.4 0.0 all-gather.5.cloned.1.call-update
  8.4 0.0 all-gather.3.cloned.1.call-start
  8.4 0.7 all-gather.3.cloned.1.call-update
  9.1 0.0 reduce-scatter.5.cloned.1.call-start
  9.2 57.1 %all-gather.5.cloned.1.call-done = bf16[8,12,128,128]{3,0,1,2:T(8,128)(2,1)} async-done(((bf16[8,12,8,128]{3,0,1,2:T(8,128)(2,1)}), bf16[8,12,128,128]{3,0,1,2:T(8,128)(2,1)}) %all-gather.5.cloned.1.call-update) | async-done | bytes 3145744 | tf_op jit(solution)/shard_map/all_gather | solution.py:18
  66.3 5.0 %copy.21 = bf16[8,12,128,128]{2,3,1,0:T(8,128)(2,1)} copy(bf16[8,12,128,128]{3,0,1,2:T(8,128)(2,1)} %all-gather.5.cloned.1.call-done) | data formatting | bytes 6291456 | tf_op jit(solution)/shard_map/all_gather | solution.py:18
  71.3 9.8 %fusion = f32[8,128,1536]{2,1,0:T(8,128)} fusion(bf16[8,128,1536]{1,2,0:T(8,128)(2,1)} %bitcast.26, bf16[1536,1536]{1,0:T(8,128)(2,1)} %param.8), kind=kOutput, calls=%fused_computation | convolution fusion | flops 4831838208 | bytes 14155776 | tf_op jit(solution)/shard_map/dot_general | solution.py:23
  81.1 0.0 reduce-scatter.5.cloned.1.call-update
  81.1 0.0 reduce-scatter.3.cloned.1.call-start
  81.2 27.7 %all-gather.3.cloned.1.call-done = bf16[8,192,8,128]{3,2,1,0:T(8,128)(2,1)} async-done(((bf16[8,12,8,128]{3,2,1,0:T(8,128)(2,1)}), bf16[8,192,8,128]{3,2,1,0:T(8,128)(2,1)}) %all-gather.3.cloned.1.call-update) | async-done | bytes 3145744 | tf_op jit(solution)/shard_map/all_gather | solution.py:11
  108.9 5.8 %dot_general.10 = bf16[8,192,1024]{2,1,0:T(8,128)(2,1)} reshape(bf16[8,192,8,128]{3,2,1,0:T(8,128)(2,1)} %all-gather.3.cloned.1.call-done) | data formatting | bytes 6291456 | tf_op jit(solution)/shard_map/dot_general | solution.py:14
  114.7 0.0 copy-done
  114.7 7.9 %fusion.2 = f32[8,192,1024]{2,0,1:T(8,128)} fusion(bf16[8,192,1024]{2,1,0:T(8,128)(2,1)} %dot_general.10, bf16[1024,1024]{1,0:T(8,128)(2,1)S(1)} %copy-done), kind=kOutput, calls=%fused_computation.2 | convolution fusion | flops 3221225472 | bytes 11534336 | tf_op jit(solution)/shard_map/dot_general | solution.py:14
  122.6 0.0 copy-start.2
  122.6 0.0 copy-start.1
  122.6 0.0 copy-start.3
  122.6 0.0 reduce-scatter.3.cloned.1.call-update
  122.7 0.6 copy-done.2
  123.3 0.1 dynamic_slice.6
  123.4 0.0 copy-done.1
  123.4 0.1 dynamic_slice.7
  123.4 0.0 copy-done.3
  123.4 0.2 select_reduce_fusion
  123.6 0.1 broadcast_add_fusion
  123.7 0.1 broadcast_subtract_fusion
  123.8 49.4 %reduce-scatter.5.cloned.1.call-done = f32[8,8,1536]{2,1,0:T(8,128)} async-done(((f32[8,128,1536]{2,1,0:T(8,128)}), f32[8,8,1536]{2,1,0:T(8,128)}) %reduce-scatter.5.cloned.1.call-update) | async-done | bytes 393232 | tf_op jit(solution)/shard_map/reduce_scatter | solution.py:25
  173.2 90.8 %reduce-scatter.3.cloned.1.call-done = f32[8,12,1024]{2,0,1:T(8,128)} async-done(((f32[8,192,1024]{2,0,1:T(8,128)}), f32[8,12,1024]{2,0,1:T(8,128)}) %reduce-scatter.3.cloned.1.call-update) | async-done | bytes 393232 | tf_op jit(solution)/shard_map/reduce_scatter | solution.py:16
  264.0 1.3 fusion.5
  265.2 0.8 copy.24
Async XLA Ops:
  6.5 108.1 %copy-start = (bf16[1024,1024]{1,0:T(8,128)(2,1)S(1)}, bf16[1024,1024]{1,0:T(8,128)(2,1)}, u32[]{:S(2)}) copy-start(bf16[1024,1024]{1,0:T(8,128)(2,1)} %param.7) | copy-start | bytes 6291460
  6.5 59.8 %all-gather.5.cloned.1.call-start = ((), (), s32[]{:S(2)}) async-start(), calls=%async_computation.4 | async-start | bytes 3342336 | tf_op jit(solution)/shard_map/all_gather | solution.py:18
  8.4 100.5 %all-gather.3.cloned.1.call-start = ((), (), s32[]{:S(2)}) async-start(), calls=%async_computation.2 | async-start | bytes 3342336 | tf_op jit(solution)/shard_map/all_gather | solution.py:11
  9.1 164.1 %reduce-scatter.5.cloned.1.call-start = ((), (), s32[]{:S(2)}) async-start(), calls=%async_computation.5 | async-start | bytes 6684672 | tf_op jit(solution)/shard_map/reduce_scatter | solution.py:25
  81.1 182.9 %reduce-scatter.3.cloned.1.call-start = ((), (), s32[]{:S(2)}) async-start(), calls=%async_computation.3 | async-start | bytes 6684672 | tf_op jit(solution)/shard_map/reduce_scatter | solution.py:16
  122.6 0.7 copy-start.2
  122.6 0.7 copy-start.1
  122.6 0.8 copy-start.3
Sparse Core Ops, SparseCore 0:
  9.8 56.4 all-gather.4
  68.2 40.6 all-gather.2
  111.5 61.7 reduce-scatter.4
  176.8 87.1 reduce-scatter.2
where the time goes:
time: 273 us
  waiting for transfers between devices  226 us (83%)
  matrix products  17.7 us (6%)
  local copies, waits for them, and re-layouts  14.1 us (5%)
  between operations  13.1 us (5%)
    reduce_scatter x1, waiting for transfers between devices, shards(): lax.psum_scatter(ladder, 'red', scatter_dimension=1, tiled=True)  90.8 us
    all_gather x1, waiting for transfers between devices, shards(): shard_piece = lax.all_gather(amplitudes, 'red', axis=2, tiled=True)  57.1 us
    reduce_scatter x1, waiting for transfers between devices, shards(): lax.psum_scatter(cycle_term, 'blk', scatter_dimension=1, tiled=True)  49.4 us
    all_gather x1, waiting for transfers between devices, shards(): shard_piece = lax.all_gather(amplitudes, 'blk', axis=1, tiled=True)  27.7 us
    dot_general x1, matrix products, shards(): product = jnp.dot(operand, cycle_ints, preferred_element_type=jnp.float32)  9.79 us
    dot_general x1, matrix products, shards(): jnp.dot(flattened, ladder_ints, preferred_element_type=jnp.float32)  7.95 us
    dot_general x1, local copies, waits for them, and re-layouts, shards(): jnp.dot(flattened, ladder_ints, preferred_element_type=jnp.float32)  5.78 us
  transfers between devices with their start and end apart: 4, of which 4 were waited for; matrix products, arithmetic and copies ran while one was open for 11% of the time, Pallas kernels for 0%

commit v1 on v0

--- a/solution.py
+++ b/solution.py
@@ -8,7 +8,9 @@
     slab_rows, occ_local, vir_local, virt_width = amplitudes.shape
     occ_all = occ_local * lax.axis_size("blk")
     occ_red = occ_all // lax.axis_size("red")
-    shard_piece = lax.all_gather(amplitudes, "blk", axis=1, tiled=True)
+    shard_piece = jnp.concatenate(
+        lax.all_to_all(jnp.stack([amplitudes] * lax.axis_size("blk")), "blk", 0, 0), axis=1
+    )
     row_count = shard_piece.shape[1]
     flattened = shard_piece.reshape(slab_rows * row_count, vir_local * virt_width)
     product = jnp.dot(flattened, ladder_ints, preferred_element_type=jnp.float32)

time: 273 us -> 301 us (1.10)
  blocking collectives: 0 us -> 97.8 us
  waiting for transfers between devices: 226 us -> 152 us
  local copies, waits for them, and re-layouts: 14.1 us -> 18.2 us
    all_to_all x0 -> x1, blocking collectives: none -> 97.8 us  [shards(): lax.all_to_all(jnp.stack([amplitudes] * lax.axis_size('blk')), 'blk', 0, 0)]
    reduce_scatter x1, waiting for transfers between devices: 49.4 us -> 4.54 us  [shards(): lax.psum_scatter(cycle_term, 'blk', scatter_dimension=1, tiled=True)]
    all_gather x1 -> x0, waiting for transfers between devices: 27.7 us -> none  [shards(): shard_piece = lax.all_gather(amplitudes, 'blk', axis=1, tiled=True)]
    dot_general x1 -> x2, local copies, waits for them, and re-layouts: 5.78 us -> 8.39 us  [shards(): jnp.dot(flattened, ladder_ints, preferred_element_type=jnp.float32)]
  transfers between devices with their start and end apart: 4 -> 3, of which waited for: 4 -> 3; matrix products, arithmetic and copies ran while one was open for 11% -> 6% of each run, Pallas kernels for 0% -> 0%
where the time goes in v1:
time: 301 us; the launch traced here: 300 us
  waiting for transfers between devices  152 us (50%)
  blocking collectives  97.8 us (32%)
  local copies, waits for them, and re-layouts  18.2 us (6%)
  matrix products  17 us (6%)
  between operations  13.1 us (4%)
    all_to_all x1, blocking collectives, shards(): lax.all_to_all(jnp.stack([amplitudes] * lax.axis_size('blk')), 'blk', 0, 0)  97.8 us
    reduce_scatter x1, waiting for transfers between devices, shards(): lax.psum_scatter(ladder, 'red', scatter_dimension=1, tiled=True)  89.8 us
    all_gather x1, waiting for transfers between devices, shards(): shard_piece = lax.all_gather(amplitudes, 'red', axis=2, tiled=True)  57.9 us
    dot_general x1, matrix products, shards(): product = jnp.dot(operand, cycle_ints, preferred_element_type=jnp.float32)  9.79 us
    dot_general x2, local copies, waits for them, and re-layouts, shards(): jnp.dot(flattened, ladder_ints, preferred_element_type=jnp.float32)  8.39 us
    dot_general x1, matrix products, shards(): jnp.dot(flattened, ladder_ints, preferred_element_type=jnp.float32)  7.26 us
  transfers between devices with their start and end apart: 3, of which 3 were waited for; matrix products, arithmetic and copies ran while one was open for 6% of the time, Pallas kernels for 0%

profile of v1, /device:TPU:1, one launch (start us, length us, event | category | flops | bytes accessed | tf_op | source)
XLA Modules:
  0.0 300.1 jit_solution(4318035991805836494)
XLA Ops:
  6.5 0.0 copy-start
  6.5 0.0 all-gather.2.cloned.1.call-start
  6.5 1.8 copy.22
  8.4 0.0 all-gather.2.cloned.1.call-update
  8.4 0.0 reduce-scatter.5.cloned.1.call-start
  8.4 57.9 %all-gather.2.cloned.1.call-done = bf16[8,12,128,128]{3,0,1,2:T(8,128)(2,1)} async-done(((bf16[8,12,8,128]{3,0,1,2:T(8,128)(2,1)}), bf16[8,12,128,128]{3,0,1,2:T(8,128)(2,1)}) %all-gather.2.cloned.1.call-update) | async-done | bytes 3145744 | tf_op jit(solution)/shard_map/all_gather | solution.py:20
  66.3 4.9 %copy.23 = bf16[8,12,128,128]{2,3,1,0:T(8,128)(2,1)} copy(bf16[8,12,128,128]{3,0,1,2:T(8,128)(2,1)} %all-gather.2.cloned.1.call-done) | data formatting | bytes 6291456 | tf_op jit(solution)/shard_map/all_gather | solution.py:20
  71.3 9.8 %fusion = f32[8,128,1536]{2,1,0:T(8,128)} fusion(bf16[8,128,1536]{1,2,0:T(8,128)(2,1)} %bitcast.31, bf16[1536,1536]{1,0:T(8,128)(2,1)} %param.8), kind=kOutput, calls=%fused_computation | convolution fusion | flops 4831838208 | bytes 14155776 | tf_op jit(solution)/shard_map/dot_general | solution.py:25
  81.0 0.0 copy-start.1
  81.0 0.0 reduce-scatter.5.cloned.1.call-update
  81.1 0.0 reduce-scatter.3.cloned.1.call-start
  81.1 0.9 copy-done.1
  82.0 0.6 stack.2
  82.6 97.8 %all_to_all.5 = bf16[16,8,12,8,128]{4,3,2,1,0:T(8,128)(2,1)S(1)} all-to-all(bf16[16,8,12,8,128]{4,3,2,1,0:T(8,128)(2,1)S(1)} %stack.2), channel_id=1, replica_groups=mesh['blk'=16,'red'=16] {'blk'}, dimensions={0} | all-to-all | bytes 6291456 | tf_op jit(solution)/shard_map/all_to_all | solution.py:12
  180.4 2.6 copy.30
  182.9 5.8 %reshape.65 = bf16[8,192,1024]{2,0,1:T(8,128)(2,1)} reshape(bf16[8,16,12,8,128]{4,3,0,2,1:T(8,128)(2,1)} %copy.30) | data formatting | bytes 6291456 | tf_op jit(solution)/shard_map/dot_general | solution.py:16
  188.8 0.0 copy-done
  188.8 7.3 %fusion.2 = f32[8,192,1024]{2,0,1:T(8,128)} fusion(bf16[8,192,1024]{2,0,1:T(8,128)(2,1)} %reshape.65, bf16[1024,1024]{1,0:T(8,128)(2,1)S(1)} %copy-done), kind=kOutput, calls=%fused_computation.2 | convolution fusion | flops 3221225472 | bytes 11534336 | tf_op jit(solution)/shard_map/dot_general | solution.py:16
  196.0 0.0 copy-start.2
  196.0 0.0 copy-start.3
  196.0 0.0 copy-start.4
  196.0 0.0 reduce-scatter.3.cloned.1.call-update
  196.1 0.6 copy-done.2
  196.7 0.1 dynamic_slice.7
  196.8 0.0 copy-done.3
  196.8 0.1 dynamic_slice.6
  196.8 0.0 copy-done.4
  196.8 0.2 select_reduce_fusion
  197.0 0.1 broadcast_add_fusion
  197.1 0.1 broadcast_subtract_fusion
  197.2 4.5 %reduce-scatter.5.cloned.1.call-done = f32[8,8,1536]{2,1,0:T(8,128)} async-done(((f32[8,128,1536]{2,1,0:T(8,128)}), f32[8,8,1536]{2,1,0:T(8,128)}) %reduce-scatter.5.cloned.1.call-update) | async-done | bytes 393232 | tf_op jit(solution)/shard_map/reduce_scatter | solution.py:27
  201.7 89.8 %reduce-scatter.3.cloned.1.call-done = f32[8,12,1024]{2,0,1:T(8,128)} async-done(((f32[8,192,1024]{2,0,1:T(8,128)}), f32[8,12,1024]{2,0,1:T(8,128)}) %reduce-scatter.3.cloned.1.call-update) | async-done | bytes 393232 | tf_op jit(solution)/shard_map/reduce_scatter | solution.py:18
  291.5 1.3 fusion.4
  292.8 0.8 copy.26
Async XLA Ops:
  6.5 182.2 %copy-start = (bf16[1024,1024]{1,0:T(8,128)(2,1)S(1)}, bf16[1024,1024]{1,0:T(8,128)(2,1)}, u32[]{:S(2)}) copy-start(bf16[1024,1024]{1,0:T(8,128)(2,1)} %param.7) | copy-start | bytes 6291460
  6.5 59.8 %all-gather.2.cloned.1.call-start = ((), (), s32[]{:S(2)}) async-start(), calls=%async_computation.4 | async-start | bytes 3342336 | tf_op jit(solution)/shard_map/all_gather | solution.py:20
  8.4 193.3 %reduce-scatter.5.cloned.1.call-start = ((), (), s32[]{:S(2)}) async-start(), calls=%async_computation.5 | async-start | bytes 6684672 | tf_op jit(solution)/shard_map/reduce_scatter | solution.py:27
  81.0 0.9 copy-start.1
  81.1 210.5 %reduce-scatter.3.cloned.1.call-start = ((), (), s32[]{:S(2)}) async-start(), calls=%async_computation.3 | async-start | bytes 6684672 | tf_op jit(solution)/shard_map/reduce_scatter | solution.py:18
  196.0 0.7 copy-start.2
  196.0 0.8 copy-start.3
  196.0 0.8 copy-start.4
Sparse Core Ops, SparseCore 0:
  9.8 56.4 all-gather.1
  81.2 120.4 reduce-scatter.4
  205.4 86.0 reduce-scatter.2
